TPU v7x, 32 devices: a whole 2x2x4 slice. The times are simulated.
32 devices in a mesh: fsdp: 32 (over z, y, x, core).
Axes of the slice: x: 2, y: 2, z: 4, core: 2. Of those that a mesh axis runs over, the one named last changes fastest.
Arguments:
- characters: bfloat16 [2, 8192, 768], P(None, 'fsdp'), may hold values from -6 to 6
- segment_ids: int32 [2, 8192], P(None, 'fsdp'), may hold values from 0 to 31, never falling along the last dimension, each value on 1 to 1024 neighbouring positions
- cotangent: bfloat16 [2, 2048, 768], P(None, 'fsdp'), may hold values from -6 to 6
- local_params: bfloat16 [7087104], P('fsdp'), may hold values from -3 to 3, as said below
- conv_params: bfloat16 [2361600], P('fsdp'), may hold values from -3 to 3, as said below
Outputs:
- molecules: bfloat16 [2, 2048, 768], P(None, 'fsdp')
- char_grads: float32 [2, 8192, 768], P(None, 'fsdp')
- local_grads: float32 [7087104], P('fsdp')
- conv_grads: float32 [2361600], P('fsdp')
Inputs may be any that keep to these rules, and one draw needn't show every extreme that they name: `local_params`: holds the layer's parameters flattened in the order of the first step (matrices row-major), the last 0 entries being padding that no output reads. `conv_params`: holds Wc row-major, then bc, g3, s3, the last 0 entries being padding that no output reads.
All inputs are finite; a program needn't handle non-finite values.
Results may differ from a plain program's by a relative error of at most 0.014.
Values may be sent and summed in bfloat16 or wider, within the bound.
A program may use at most 256 MiB of HBM per device.

v0:
```python
import functools
import math
from types import SimpleNamespace

import jax
import jax.numpy as jnp
from jax import lax
from jax.experimental import pallas as pl
from jax.experimental.pallas import tpu as pltpu
from jax.sharding import PartitionSpec as P

MESH = pl.DeviceIdType.MESH
F32, BF16 = jnp.float32, jnp.bfloat16
D, FF, HEADS, WINDOW, RATE, MICRO, HEAD_SIZE = 768, 3072, 12, 128, 4, 2, 64
LOCAL_COUNT, CONV_COUNT = 7087104, 2361600
LANE = 128
UNIT = 1152
EPS = EPSILON = 1e-05


DC = D // LANE
FC = FF // LANE
VB1, VG1, VS1, VBQ, VBV, VBO, VG2, VS2, VB2 = 0, 24, 30, 36, 42, 48, 54, 60, 66
VBC, VG3, VS3 = 78, 84, 90
QKV_ROW, O_ROW, W1_ROW, W2_ROW = 0, 18 * D, 24 * D, 48 * D

def nn(a, b): return jnp.dot(a, b, preferred_element_type=F32)
def nt(a, b): return lax.dot_general(a, b, (((1,), (1,)), ((), ())), preferred_element_type=F32)
def tn(a, b): return lax.dot_general(a, b, (((0,), (0,)), ((), ())), preferred_element_type=F32)

def loop(n, fn, unroll=1):
    def body(i, _):
        fn(i)
        return 0
    lax.fori_loop(0, n, body, 0, unroll=unroll)

def span(lo, hi, n, fn, unroll=1):
    hi = n if hi is None else hi
    def body(i, _):
        fn(i)
        return 0
    lax.fori_loop(lo, hi, body, 0, unroll=unroll)

def at(i, size): return pl.ds(pl.multiple_of(i * size, size), size)

def vec(r, row, blocks=DC):
    return jnp.concatenate([r.vecs[row + i:row + i + 1, :] for i in range(blocks)], axis=1)

def put(r, row, value):
    for i in range(value.shape[1] // LANE):
        r.vgrad[row + i:row + i + 1, :] = value[:, i * LANE:(i + 1) * LANE]

def add_to(r, row, value):
    for i in range(value.shape[1] // LANE):
        r.vgrad[row + i:row + i + 1, :] += value[:, i * LANE:(i + 1) * LANE]

def normal(v):
    mean = jnp.mean(v, axis=-1, keepdims=True)
    cen = v - mean
    var = jnp.mean(cen * cen, axis=-1, keepdims=True)
    s = lax.rsqrt(var + EPS)
    return cen * s, s

def normal_back(dn, nrm, s):
    return s * (dn - jnp.mean(dn, axis=-1, keepdims=True) - nrm * jnp.mean(dn * nrm, axis=-1, keepdims=True))

def colsum(v): return jnp.sum(v, axis=0, keepdims=True)

def gelu_both(h):
    cdf = 0.5 + 0.5 * lax.erf(h * (0.5 ** 0.5))
    pdf = jnp.exp(-0.5 * h * h) * (1.0 / math.sqrt(2 * math.pi))
    return h * cdf, cdf + h * pdf

RB = 64
def forward_norm(r):
    g1, s1 = vec(r, VG1), vec(r, VS1)
    def f(i):
        nrm, _ = normal(r.x[at(i, RB), :].astype(F32))
        r.a[at(i, RB), :] = (nrm * g1 + s1).astype(BF16)
    loop(r.rows // RB, f, 2)

def forward_qkv(r, lo=0, hi=9):
    bias = jnp.concatenate([vec(r, VBQ), jnp.zeros((1, D), F32), vec(r, VBV)], axis=1)
    for i in range(18):
        r.bias[i:i + 1, :] = bias[:, i * LANE:(i + 1) * LANE]
    def f(i):
        b = jnp.concatenate([r.bias[pl.ds(2 * i, 1), :], r.bias[pl.ds(2 * i + 1, 1), :]], axis=1)
        r.P[:, at(i, 256)] = (nn(r.a[...], r.wqkv[:, at(i, 256)]) + b).astype(BF16)
    span(lo, hi, 9, f, 3)

def halves(v):
    lo = lax.broadcasted_iota(jnp.int32, v.shape, 1) < 64
    w = v.astype(F32)
    z = jnp.zeros_like(w)
    return jnp.concatenate([jnp.where(lo, w, z), jnp.where(lo, z, w)], axis=0).astype(BF16)

def pick(v):
    lo = lax.broadcasted_iota(jnp.int32, (WINDOW, LANE), 1) < 64
    return jnp.where(lo, v[:WINDOW], v[WINDOW:])

def heads_of(r, i):
    w = i // DC
    hp = lax.rem(i, DC)
    rows = at(w, WINDOW)
    return w, rows, at(hp, LANE), at(hp + DC, LANE), at(hp + 2 * DC, LANE)

def same_segment(r):
    per = r.seg.shape[1] // WINDOW
    for w in range(r.rows // WINDOW):
        ids = r.seg[w // per:w // per + 1, w % per * WINDOW:(w % per + 1) * WINDOW].astype(F32)
        wide = jnp.broadcast_to(ids, (WINDOW, WINDOW))
        r.same[w] = (wide == wide.T).astype(F32)

def forward_attention(r, lo=0, hi=24):
    def f(i):
        w, rows, cq, ck, cv = heads_of(r, i)
        q2 = halves(r.P[rows, cq])
        s = nt(q2, r.P[rows, ck]) * 0.125
        same = r.same[w]
        same2 = jnp.concatenate([same, same], axis=0) > 0.5
        s = jnp.where(same2, s, -1e30)
        e = jnp.exp(s - jnp.max(s, axis=-1, keepdims=True))
        p = (e / jnp.sum(e, axis=-1, keepdims=True)).astype(BF16)
        r.p[i] = p
        r.ctx[rows, cq] = pick(nn(p, r.P[rows, cv])).astype(BF16)
    span(lo, hi, 24, f, 4)

def forward_out(r):
    bo = vec(r, VBO)
    for i in range(3):
        c = slice(i * 256, (i + 1) * 256)
        r.y1[:, c] = r.x[:, c].astype(F32) + nn(r.ctx[...], r.wo[:, c]) + bo[:, c]
    g2, s2 = vec(r, VG2), vec(r, VS2)
    def f(i):
        nrm, _ = normal(r.y1[at(i, RB), :])
        r.c[at(i, RB), :] = (nrm * g2 + s2).astype(BF16)
    loop(r.rows // RB, f, 2)

def forward_up(r, lo=0, hi=12):
    def f(i):
        b = jnp.concatenate([r.vecs[pl.ds(VB1 + 2 * i, 1), :], r.vecs[pl.ds(VB1 + 2 * i + 1, 1), :]], axis=1)
        h = nn(r.c[...], r.w1[:, at(i, 256)]) + b
        hid, slope = gelu_both(h)
        r.hid[:, at(i, 256)] = hid.astype(BF16)
        r.slope[:, at(i, 256)] = slope.astype(BF16)
    span(lo, hi, 12, f, 2)

def forward_down(r):
    b2 = vec(r, VB2)
    for i in range(3):
        c = slice(i * 256, (i + 1) * 256)
        v = r.y1[:, c] + nn(r.hid[...], r.w2[:, c]) + b2[:, c]
        r.ys[2 * i] = v[:, :LANE]
        r.ys[2 * i + 1] = v[:, LANE:]
    for j in range(RATE):
        for c in range(DC):
            r.u[j * r.mols:(j + 1) * r.mols, c * LANE:(c + 1) * LANE] = r.ys[c, pl.ds(j, r.mols, stride=RATE), :].astype(BF16)

def forward_conv(r):
    z = vec(r, VBC)
    for j in range(RATE):
        z = z + nn(r.u[j * r.mols:(j + 1) * r.mols, :], r.wc[j * D:(j + 1) * D, :])
    w, slope = gelu_both(z)
    nrm, s = normal(w)
    r.mol[...] = (nrm * vec(r, VG3) + vec(r, VS3)).astype(BF16)
    t = r.cot[...].astype(F32)
    put(r, VG3, colsum(t * nrm))
    put(r, VS3, colsum(t))
    dw = normal_back(t * vec(r, VG3), nrm, s)
    dz = (dw * slope).astype(BF16)
    r.dz[...] = dz
    put(r, VBC, colsum(dz.astype(F32)))

def emit_flat(r, dst, row0, tile, base=0):
    k, m = tile.shape[0], tile.shape[1] // LANE
    for c in range(m):
        r.scr[pl.ds(base + c, k, stride=m), :] = tile[:, c * LANE:(c + 1) * LANE]
    dst[pl.ds(pl.multiple_of(row0, 16), k * m), :] = r.scr[base:base + k * m, :].astype(BF16)

def emit_pair(r, dst, row0, lhs, rhs):
    tiles = [tn(lhs(h), rhs) for h in (0, 1)]
    for h in (0, 1): emit_flat(r, dst, row0 + h * 256 * DC, tiles[h], h * 256 * DC)

def grad_conv_weight(r, j):
    for i in range(3):
        emit_flat(r, r.gc, (j * D + i * 256) * DC, tn(r.u[j * r.mols:(j + 1) * r.mols, i * 256:(i + 1) * 256], r.dz[...]), i % 2 * 256 * DC)

def back_conv(r):
    for j in range(RATE):
        v = nt(r.dz[...], r.wc[j * D:(j + 1) * D, :])
        for c in range(DC):
            r.ys[c, pl.ds(j, r.mols, stride=RATE), :] = v[:, c * LANE:(c + 1) * LANE]
    for c in range(DC):
        v = r.ys[c]
        r.u[:, c * LANE:(c + 1) * LANE] = v.astype(BF16)
        put(r, VB2 + c, colsum(v))

def grad_down_weight(r, lo=0, hi=12):
    span(lo // 2, hi // 2, 6, lambda i: emit_pair(r, r.gl, W2_ROW + i * 512 * DC, lambda h: r.hid[:, pl.ds(pl.multiple_of(i * 512 + h * 256, 256), 256)], r.u[...]))

def back_down(r, lo=0, hi=12):
    def f(i):
        cols = [at(2 * i + h, 256) for h in (0, 1)]
        slopes = [r.slope[:, c] for c in cols]
        outs = [(nt(r.u[...], r.w2[c, :]) * s.astype(F32)).astype(BF16) for c, s in zip(cols, slopes)]
        for h, (c, dh) in enumerate(zip(cols, outs)):
            r.slope[:, c] = dh
            s = colsum(dh.astype(F32))
            r.vgrad[pl.ds(VB1 + 4 * i + 2 * h, 1), :] = s[:, :LANE]
            r.vgrad[pl.ds(VB1 + 4 * i + 2 * h + 1, 1), :] = s[:, LANE:]
    span(lo // 2, hi // 2, 6, f)

def grad_up_weight(r, lo=0, hi=6):
    span(lo, hi, 6, lambda i: emit_flat(r, r.gl, W1_ROW + i * 128 * FC, tn(r.c[:, at(i, 128)], r.slope[...])))

def fold(v):
    out = v[0:8]
    for i in range(1, v.shape[0] // 8):
        out = out + v[i * 8:(i + 1) * 8]
    return out

def row_sums(r, fn, count):
    def body(i, acc):
        return tuple(a + fold(v) for a, v in zip(acc, fn(at(i, RB))))
    acc = lax.fori_loop(0, r.rows // RB, body, tuple(jnp.zeros((8, D), F32) for _ in range(count)), unroll=2)
    return [colsum(a) for a in acc]

def back_up(r):
    for i in range(3):
        r.dc[:, i * 256:(i + 1) * 256] = nt(r.slope[...], r.w1[i * 256:(i + 1) * 256, :])
    g2 = vec(r, VG2)
    def f(rows):
        dc = r.dc[rows, :]
        nrm, s = normal(r.y1[rows, :])
        dy2 = jnp.concatenate([r.ys[c, rows, :] for c in range(DC)], axis=1)
        dy1 = dy2 + normal_back(dc * g2, nrm, s)
        r.dc[rows, :] = dy1
        r.u[rows, :] = dy1.astype(BF16)
        return dc * nrm, dc, dy1
    sums = row_sums(r, f, 3)
    put(r, VG2, sums[0])
    put(r, VS2, sums[1])
    put(r, VBO, sums[2])

def grad_out_weight(r):
    for i in range(3):
        emit_flat(r, r.gl, O_ROW + i * 256 * DC, tn(r.ctx[:, i * 256:(i + 1) * 256], r.u[...]), i % 2 * 256 * DC)

def back_out(r):
    for i in range(3):
        r.c[:, i * 256:(i + 1) * 256] = nt(r.u[...], r.wo[i * 256:(i + 1) * 256, :]).astype(BF16)

AG = 6
def back_attention(r, lo=0, hi=None):
    def f(i):
        where = [heads_of(r, i * AG + j) for j in range(AG)]
        loads = [(r.c[rows, cq], r.P[rows, cq], r.P[rows, ck], r.P[rows, cv], r.p[i * AG + j]) for j, (w, rows, cq, ck, cv) in enumerate(where)]
        outs = []
        for do, q, k, v, pb in loads:
            do2, q2 = halves(do), halves(q)
            p = pb.astype(F32)
            dp = nt(do2, v)
            ds = (p * (dp - jnp.sum(p * dp, axis=-1, keepdims=True))).astype(BF16)
            outs.append((pick(nn(ds, k)) * 0.125, tn(ds, q2) * 0.125, tn(pb, do2)))
        for (w, rows, cq, ck, cv), (dq, dk, dv) in zip(where, outs):
            r.P[rows, cq] = dq.astype(BF16)
            r.P[rows, ck] = dk.astype(BF16)
            r.P[rows, cv] = dv.astype(BF16)
    span(lo, hi, r.rows // WINDOW * DC // AG, f)

def grad_qkv_weight(r):
    for c in range(DC):
        r.vgrad[VBQ + c:VBQ + c + 1, :] = colsum(r.P[:, c * LANE:(c + 1) * LANE].astype(F32))
        r.vgrad[VBV + c:VBV + c + 1, :] = colsum(r.P[:, 2 * D + c * LANE:2 * D + (c + 1) * LANE].astype(F32))
    loop(6, lambda i: emit_flat(r, r.gl, QKV_ROW + i * 128 * 18, tn(r.a[:, at(i, 128)], r.P[...])))

def back_qkv(r):
    for i in range(3):
        r.y1[:, i * 256:(i + 1) * 256] = nt(r.P[...], r.wqkv[i * 256:(i + 1) * 256, :])
    g1 = vec(r, VG1)
    def f(rows):
        da = r.y1[rows, :]
        nrm, s = normal(r.x[rows, :].astype(F32))
        r.dc[rows, :] = r.dc[rows, :] + normal_back(da * g1, nrm, s)
        return da * nrm, da
    sums = row_sums(r, f, 2)
    put(r, VG1, sums[0])
    put(r, VS1, sums[1])

def state_shapes(rows):
    mols = rows // RATE
    V = pltpu.VMEM
    return dict(
        same=V((rows // WINDOW, WINDOW, WINDOW), F32), a=V((rows, D), BF16), P=V((rows, 3 * D), BF16), p=V((rows // WINDOW * DC, 2 * WINDOW, LANE), BF16),
        ctx=V((rows, D), BF16), y1=V((rows, D), F32), c=V((rows, D), BF16), slope=V((rows, FF), BF16), hid=V((rows, FF), BF16),
        ys=V((DC, rows, LANE), F32), u=V((rows, D), BF16), dz=V((mols, D), BF16), dc=V((rows, D), F32),
        scr=V((128 * FC, LANE), F32), bias=V((24, LANE), F32), vecs=V((96, LANE), F32))


class Geo:
    def __init__(self, n, local_shard, conv_shard):
        self.n = n
        self.local_shard, self.conv_shard = local_shard, conv_shard
        self.Z = n // 8
        self.RL = (12 * D * D) // LANE // n
        self.RC = (4 * D * D) // LANE // n
        self.dl = local_shard - self.RL * LANE
        self.dc = conv_shard - self.RC * LANE
        self.HL = -(-(self.dl * n) // (8 * LANE)) * 8
        self.HC = -(-(self.dc * n) // (8 * LANE)) * 8
        self.XL = -(-local_shard // (8 * LANE)) * 8
        self.XC = -(-conv_shard // (8 * LANE)) * 8

def where_am_i():
    me = lax.axis_index("fsdp")
    core = lax.rem(me, 2)
    bx = lax.rem(me // 2, 2)
    by = lax.rem(me // 4, 2)
    z = me // 8
    sib = me + 1 - 2 * core
    xn = me + 2 - 4 * bx
    yn = me + 4 - 8 * by
    first = xn + core * (yn - xn)
    second = yn + core * (xn - yn)
    return me, core, z, sib, first, second

def realign(out_ref, out_base, lo, hi, x_ref, shift, step=16):
    q = shift // LANE
    r = lax.rem(shift, LANE)
    turn = lax.rem(LANE - r, LANE)
    lane = lax.broadcasted_iota(jnp.int32, (step, LANE), 1)
    keep = lane < (LANE - r)
    def body(i, _):
        low = x_ref[pl.ds(q + i * step, step), :]
        high = x_ref[pl.ds(q + i * step + 1, step), :]
        val = jnp.where(keep, pltpu.roll(low, turn, 1), pltpu.roll(high, turn, 1))
        out_ref[pl.ds(pl.multiple_of(out_base + i * step, step), step), :] = val.astype(out_ref.dtype)
        return 0
    many = max(u for u in (1, 2, 3, 4, 5, 6, 8) if (hi - lo) // step % u == 0)
    lax.fori_loop(lo // step, hi // step, body, 0, unroll=many)

def widen(dst_ref, dst_base, src_ref, rows):
    step = 248 if rows % 248 == 0 else 8
    for i in range(rows // step):
        dst_ref[dst_base + i * step:dst_base + (i + 1) * step, :] = src_ref[i * step:(i + 1) * step, :].astype(F32)

def convert_unit(src_ref, base, w_ref, krow, cols, scr):
    groups = UNIT // (16 * cols)
    def body(g, _):
        scr[0:16 * cols, :] = src_ref[pl.ds(pl.multiple_of(base + g * 16 * cols, 16), 16 * cols), :].astype(F32)
        for cc in range(cols):
            v = scr[pl.ds(cc, 16, stride=cols), :]
            w_ref[pl.ds(pl.multiple_of(krow + g * 16, 16), 16), cc * LANE:(cc + 1) * LANE] = v.astype(BF16)
        return 0
    lax.fori_loop(0, groups, body, 0)


def start_gather(g):
    n, Z, geo, me, z = g.n, g.Z, g.geo, g.me, g.z
    RL, RC = geo.RL, geo.RC
    nxt = lax.rem(me + 1, n)
    bar = pltpu.get_barrier_semaphore()
    far = lax.rem(me + n + 2 * g.core - 1, n)
    for dev in (g.sib, g.first, g.second, far):
        pl.semaphore_signal(bar, inc=1, device_id=(dev,), device_id_type=MESH)
    @pl.when(z > 0)
    def _(): pl.semaphore_signal(bar, inc=1, device_id=(me - 8,), device_id_type=MESH)
    @pl.when(z < Z - 1)
    def _(): pl.semaphore_signal(bar, inc=1, device_id=(me + 8,), device_id_type=MESH)
    widen(g.xlf, geo.HL, g.xl, geo.XL)
    widen(g.xcf, geo.HC, g.xc, geo.XC)
    realign(g.fs, 0, 0, geo.HL, g.xlf, geo.local_shard, 8)
    realign(g.fs, geo.HL, 0, geo.HC, g.xcf, geo.conv_shard, 8)
    g.hb[...] = g.fs[...].astype(BF16)
    HA, HB = 96, 96
    lshift, cshift = geo.HL * LANE - geo.dl * me, geo.HC * LANE - geo.dc * me
    realign(g.gl, me * RL, HA, RL, g.xlf, lshift)
    realign(g.gc, me * RC, HB, RC, g.xcf, cshift)
    pl.semaphore_wait(bar, 4 + jnp.where(z > 0, 1, 0) + jnp.where(z < Z - 1, 1, 0))
    halo = pltpu.make_async_remote_copy(src_ref=g.hb, dst_ref=g.hr, send_sem=g.hsem.at[0], recv_sem=g.hsem.at[1], device_id=(nxt,), device_id_type=MESH)
    halo.start()
    halo.wait()
    g.xlf[0:geo.HL, :] = g.hr[0:geo.HL, :].astype(F32)
    g.xcf[0:geo.HC, :] = g.hr[geo.HL:geo.HL + geo.HC, :].astype(F32)
    realign(g.gl, me * RL, 0, HA, g.xlf, lshift)
    realign(g.gc, me * RC, 0, HB, g.xcf, cshift)
    @pl.when(me == n - 1)
    def _():
        g.tail[...] = g.hb[...]


def gather_table(g):
    Z, me, z = g.Z, g.me, g.z
    bx, by = lax.rem(me // 2, 2), lax.rem(me // 4, 2)
    one = g.core == 1
    def copy(slot, dev):
        return pltpu.make_async_remote_copy(src_ref=g.tail, dst_ref=g.tail, send_sem=g.tsem.at[slot], recv_sem=g.tsem.at[4], device_id=(dev,), device_id_type=MESH)
    right = jnp.logical_and(one, bx == 1)
    corner = jnp.logical_and(right, by == 1)
    sends = ((0, me - 8, jnp.logical_and(corner, z > 0)), (1, g.first, corner), (2, g.second, right), (3, g.sib, one))
    @pl.when(me != g.n - 1)
    def _(): copy(0, g.sib).wait_recv()
    for slot, dev, there in sends:
        @pl.when(there)
        def _(): copy(slot, dev).start()
    g.vecs[...] = g.tail[...].astype(F32)
    def finish():
        for slot, dev, there in sends:
            @pl.when(there)
            def _(): copy(slot, dev).wait_send()
    return finish


class Gather:
    def __init__(self, g, parts):
        self.g = g
        self.parts = parts
        self.size = (g.geo.RL, g.geo.RC)
        self.place = (g.gl, g.gc)

    def source(self, dz, f, s):
        g = self.g
        return g.me + 8 * dz + f * (g.first - g.me) + s * (g.second - g.me)

    def copy(self, k, p, src, dev, slot):
        g = self.g
        rows = self.size[k] // self.parts[k]
        i = p if k == 0 else self.parts[0] + p
        ref = self.place[k].at[pl.ds(pl.multiple_of(src * self.size[k] + p * rows, 16), rows)]
        return pltpu.make_async_remote_copy(src_ref=ref, dst_ref=ref, send_sem=g.ssem.at[i, slot], recv_sem=g.rsem.at[i, src], device_id=(dev,), device_id_type=MESH)

    def sends(self, o, k, p, dz):
        g, z, Z = self.g, self.g.z, self.g.Z
        f, s = {1: (0, 0), 2: (1, 0), 3: (0, 1), 4: (1, 1)}[o]
        src, zi = self.source(dz, f, s), z + dz
        out = []
        if k == 1:
            if dz >= 0: out.append((lambda: self.copy(k, p, src, g.me - 8, (o - 1) * Z + zi), z > 0))
            if dz <= 0: out.append((lambda: self.copy(k, p, src, g.me + 8, (o + 3) * Z + zi), z < Z - 1))
            if dz == 0 and o == 1: out.append((lambda: self.copy(k, p, src, g.first, 8 * Z), None))
            if dz == 0 and o <= 2: out.append((lambda: self.copy(k, p, src, g.second, 8 * Z + o), None))
            out.append((lambda: self.copy(k, p, src, g.sib, (8 + o) * Z + zi), None))
            return src, out
        if o == 1:
            if dz >= 0: out.append((lambda: self.copy(k, p, src, g.me - 8, zi), z > 0))
            if dz <= 0: out.append((lambda: self.copy(k, p, src, g.me + 8, Z + zi), z < Z - 1))
            out.append((lambda: self.copy(k, p, src, g.first, 2 * Z + zi), None))
        if o <= 2: out.append((lambda: self.copy(k, p, src, g.second, (2 + o) * Z + zi), None))
        out.append((lambda: self.copy(k, p, src, g.sib, (4 + o) * Z + zi), None))
        return src, out

    def guard(self, cond, fn):
        if cond is None: fn()
        else: pl.when(cond)(fn)

    def valid(self, dz, fn):
        z, Z = self.g.z, self.g.Z
        self.guard(None if dz == 0 else jnp.logical_and(z + dz >= 0, z + dz < Z), fn)

    def event(self, o, k, p, dz):
        def fn():
            src, sends = self.sends(o, k, p, dz)
            if o > 1 or dz != 0: self.copy(k, p, src, self.g.sib, 0).wait_recv()
            for cp, there in sends: self.guard(there, lambda cp=cp: cp().start())
        self.valid(dz, fn)

    def drain(self, o, k, p, dz):
        def fn():
            for cp, there in self.sends(o, k, p, dz)[1]: self.guard(there, lambda cp=cp: cp().wait_send())
        self.valid(dz, fn)

    def convert(self, k, dz):
        g = self.g
        per = 2 * self.size[k] // UNIT
        def fn():
            def chip_body(c, _):
                src = self.source(dz, c // 2, lax.rem(c, 2))
                for p in range(self.parts[k]): self.copy(k, p, src + g.sib - g.me, g.sib, 0).wait_recv()
                def unit(i, _):
                    t = (src // 2) * per + i
                    base = t * UNIT
                    if k == 1: convert_unit(g.gc, base, g.wc, t * 192, 6, g.scr)
                    else:
                        @pl.when(t < 12)
                        def _(): convert_unit(g.gl, base, g.wqkv, t * 64, 18, g.scr)
                        @pl.when(jnp.logical_and(t >= 12, t < 16))
                        def _(): convert_unit(g.gl, base, g.wo, (t - 12) * 192, 6, g.scr)
                        @pl.when(jnp.logical_and(t >= 16, t < 32))
                        def _(): convert_unit(g.gl, base, g.w1, (t - 16) * 48, 24, g.scr)
                        @pl.when(t >= 32)
                        def _(): convert_unit(g.gl, base, g.w2, (t - 32) * 192, 6, g.scr)
                    return 0
                lax.fori_loop(0, per, unit, 0)
                return 0
            lax.fori_loop(0, 4, chip_body, 0)
        self.valid(dz, fn)


PART = 576
RING = 4


class Scatter:
    def __init__(self, g, jobs):
        self.g = g
        self.size = (g.geo.RL, g.geo.RC)
        self.own = (g.gl, g.gc)
        self.jobs = jobs
        self.started, self.granted, self.waiting = set(), set(), []
        self.opened = self.closed = 0

    def target(self, zt, f, s):
        g = self.g
        return g.me + 8 * (zt - g.z) + f * (g.first - g.me) + s * (g.second - g.me)

    def other(self, zt, f, s): return self.target(zt, f, s) + self.g.sib - self.g.me

    def rows(self, k, t, p):
        return pl.ds(pl.multiple_of(t * self.size[k] + p * PART, 16), PART)

    def sem(self, k, p):
        return p if k == 0 else self.size[0] // PART + p

    def move(self, src, dst, send, recv, i, index, dev):
        return pltpu.make_async_remote_copy(src_ref=src, dst_ref=dst, send_sem=send.at[i, index], recv_sem=recv.at[i, index], device_id=(dev,), device_id_type=MESH)

    def at(self, k, p, t): return self.own[k].at[self.rows(k, t, p)]

    def to_sib(self, k, p, t):
        g = self.g
        return self.move(self.at(k, p, t), g.from_sib[k].at[self.rows(k, t // 2, p)], g.s_sib, g.r_sib, self.sem(k, p), t // 2, g.sib)

    def to_second(self, k, p, zt, f):
        g = self.g
        t = self.target(zt, f, 1)
        return self.move(self.at(k, p, t), self.at(k, p, t + g.sib - g.me), g.s_second, g.r_second, self.sem(k, p), 2 * zt + f, g.second)

    def to_first(self, k, p, zt):
        g = self.g
        t = self.target(zt, 1, 0)
        return self.move(self.at(k, p, t), self.at(k, p, t + g.second - g.me + g.sib - g.me), g.s_first, g.r_first, self.sem(k, p), zt, g.first)

    def down(self, k, p, zt):
        g = self.g
        return self.move(self.at(k, p, self.target(zt, 0, 0)), self.at(k, p, self.other(zt, 1, 1)), g.s_down, g.r_down, self.sem(k, p), zt, g.me - 8)

    def up(self, k, p, zt, land):
        g = self.g
        dst = (g.below_l, g.below_c)[k].at[pl.ds(p * PART, PART)] if land else self.at(k, p, self.other(zt, 1, 1))
        return self.move(self.at(k, p, self.target(zt, 0, 0)), dst, g.s_up, g.r_up, self.sem(k, p), zt, g.me + 8)

    def p0(self, k, p, zt):
        for f in (0, 1):
            for s in (0, 1):
                self.to_sib(k, p, self.other(zt, f, s)).start()
        self.started.add((k, p, zt))
        self.waiting.append((k, p, zt))

    def ticket(self, which, k, p, zt): return self.g.credit.at[which, self.sem(k, p) * self.g.Z + zt]

    def credit(self, which, k, p, zt, dev):
        pl.semaphore_signal(self.ticket(which, k, p, zt), inc=1, device_id=(dev,), device_id_type=MESH)

    def grant(self, k, p, zt):
        g = self.g
        z, Z, me = g.z, g.Z, g.me
        for f in (0, 1):
            for s in (0, 1):
                self.to_sib(k, p, self.other(zt, f, s)).wait_send()
        self.credit(0, k, p, zt, g.second)
        self.credit(1, k, p, zt, g.second)
        self.credit(2, k, p, zt, g.first)
        if zt < Z - 1:
            @pl.when(jnp.logical_and(z >= zt, z < Z - 1))
            def _(): self.credit(3, k, p, zt, me + 8)
        if zt > 1:
            @pl.when(jnp.logical_and(z < zt, z > 0))
            def _(): self.credit(4, k, p, zt, me - 8)
        self.granted.add((k, p, zt))

    def grant_all(self):
        for st in self.waiting: self.grant(*st)
        self.waiting = []

    def spend(self, which, k, p, zt): pl.semaphore_wait(self.ticket(which, k, p, zt), 1)

    def place(self, job):
        kind, (k, p, zt), x = job
        z, Z = self.g.z, self.g.Z
        if kind == "second": return None, self.target(zt, x, 1)
        if kind == "first": return None, self.target(zt, 1, 0)
        if kind == "last": return z == zt, self.target(zt, 0, 0)
        return z == (x[0] if x[1] else Z - 1 - x[0]), self.target(zt, 0, 0)

    def describe(self, job):
        kind, (k, p, zt), x = job
        g = self.g
        z, Z, me = g.z, g.Z, g.me
        if kind == "second":
            def send():
                self.spend(x, k, p, zt)
                self.to_second(k, p, zt, x).start()
            return [], [], None, send
        if kind == "first":
            def send():
                self.spend(2, k, p, zt)
                self.to_first(k, p, zt).start()
            return [self.to_second(k, p, zt, 1)], [self.at(k, p, self.other(zt, 1, 0))], None, send
        waits = [self.to_second(k, p, zt, 0), self.to_first(k, p, zt)]
        lands = [self.at(k, p, self.other(zt, 0, 0)), self.at(k, p, self.other(zt, 0, 1))]
        far = self.at(k, p, self.other(zt, 1, 1))
        if kind == "last":
            if zt < Z - 1:
                waits.append(self.down(k, p, zt))
                lands.append(far)
            if zt > 0:
                waits.append(self.up(k, p, zt, True))
                lands.append((g.below_l, g.below_c)[k].at[pl.ds(p * PART, PART)])
            return waits, lands, (g.xlf, g.xcf)[k], None
        hop, upward = x
        if hop > 0:
            waits.append(self.up(k, p, zt, False) if upward else self.down(k, p, zt))
            lands.append(far)
        here = hop if upward else Z - 1 - hop
        def send():
            if upward:
                if here + 1 < zt: self.spend(4, k, p, zt)
                self.up(k, p, zt, here + 1 == zt).start()
            else:
                self.spend(3, k, p, zt)
                self.down(k, p, zt).start()
        return waits, lands, None, send

    def guard(self, cond, fn):
        if cond is None: fn()
        else: pl.when(cond)(fn)

    def fetch(self, job, t, slot):
        g, (k, p, zt) = self.g, job[1]
        return pltpu.make_async_copy(g.from_sib[k].at[self.rows(k, t // 2, p)], g.tmp.at[slot], g.fsem.at[slot])

    def open(self, i):
        job = self.jobs[i]
        cond, t = self.place(job)
        def fn():
            self.to_sib(*job[1][:2], t).wait_recv()
            self.fetch(job, t, i % RING).start()
        self.guard(cond, fn)

    def close(self, i):
        g, job, slot = self.g, self.jobs[i], i % RING
        k, p, zt = job[1]
        cond, t = self.place(job)
        def fn():
            waits, lands, out, send = self.describe(job)
            for cp in waits: cp.wait_recv()
            self.fetch(job, t, slot).wait()
            mine = self.at(k, p, t)
            def body(b, _):
                r = pl.ds(pl.multiple_of(b * 16, 16), 16)
                acc = mine[r, :].astype(F32) + g.tmp[slot, r, :].astype(F32)
                for land in lands: acc = acc + land[r, :].astype(F32)
                if out is None: mine[r, :] = acc.astype(BF16)
                else: out[pl.ds(pl.multiple_of(p * PART + b * 16, 16), 16), :] = acc
                return 0
            lax.fori_loop(0, PART // 16, body, 0, unroll=4)
            if send is not None: send()
        self.guard(cond, fn)

    def run(self):
        i = self.closed
        step = self.jobs[i][1]
        if step not in self.granted: self.grant_all()
        while self.opened < len(self.jobs) and self.opened < i + RING and self.jobs[self.opened][1] in self.started:
            self.open(self.opened)
            self.opened += 1
        self.close(i)
        self.closed += 1

    def finish(self, k, p, zt):
        g = self.g
        for f in (0, 1): self.to_second(k, p, zt, f).wait_send()
        self.to_first(k, p, zt).wait_send()
        @pl.when(g.z > zt)
        def _(): self.down(k, p, zt).wait_send()
        @pl.when(g.z < zt)
        def _(): self.up(k, p, zt, False).wait_send()


def reduce_vectors(g):
    Z, me, z = g.Z, g.me, g.z
    core = lax.rem(me, 2)
    bx, by = lax.rem(me // 2, 2), lax.rem(me // 4, 2)
    def cp(slot, dev):
        return pltpu.make_async_remote_copy(src_ref=g.vgrad, dst_ref=g.vland.at[slot], send_sem=g.vsem.at[0], recv_sem=g.vsem.at[1 + slot], device_id=(dev,), device_id_type=MESH)
    def take(slot):
        cp(slot, g.sib).wait_recv()
        g.vgrad[...] = g.vgrad[...] + g.vland[slot]
    def give(slot, dev):
        c = cp(slot, dev)
        c.start()
        c.wait_send()
    on = core == 1
    def stage0():
        @pl.when(jnp.logical_not(on))
        def _(): give(0, g.sib)
        @pl.when(on)
        def _(): take(0)
    def stage1():
        @pl.when(jnp.logical_and(on, bx == 0))
        def _(): give(1, g.second)
        @pl.when(jnp.logical_and(on, bx == 1))
        def _(): take(1)
    def stage2():
        @pl.when(jnp.logical_and(on, jnp.logical_and(bx == 1, by == 0)))
        def _(): give(2, g.first)
        @pl.when(jnp.logical_and(on, jnp.logical_and(bx == 1, by == 1)))
        def _(): take(2)
    def stage3():
        @pl.when(jnp.logical_and(on, jnp.logical_and(bx == 1, by == 1)))
        def _():
            @pl.when(z > 0)
            def _(): take(3)
            @pl.when(z < Z - 1)
            def _(): give(3, me + 8)
    return stage0, stage1, stage2, stage3


def place_gradients(g):
    n, geo, me = g.n, g.geo, g.me
    prv = lax.rem(me + n - 1, n)
    edge = me == n - 1
    HL, HC = geo.HL, geo.HC
    skip = VBC - HL
    vectors = ((0, HL, HL), (VBC, HL + HC, HC - skip))
    def part(k):
        x, out, rows, drift = ((g.xlf, g.outl, geo.RL, geo.dl), (g.xcf, g.outc, geo.RC, geo.dc))[k]
        first, last = (0, HL) if k == 0 else (HL, HL + HC)
        cp = pltpu.make_async_remote_copy(src_ref=g.fs.at[pl.ds(first, last - first)], dst_ref=g.fr.at[pl.ds(first, last - first)],
                                          send_sem=g.hsem.at[2 + 2 * k], recv_sem=g.hsem.at[3 + 2 * k], device_id=(prv,), device_id_type=MESH)
        def begin():
            g.fs[first:last, :] = x[0:last - first, :]
            cp.start()
        split = (rows - 96) // 96 * 96
        def middle(): realign(out, 0, 0, split, x, drift * me)
        def end():
            cp.wait()
            lo, hi, count = vectors[k]
            x[rows:rows + count, :] = jnp.where(edge, g.vgrad[lo:hi, :], g.fr[first:first + count, :])
            realign(out, 0, split, out.shape[0], x, drift * me)
        return begin, middle, end
    return part(0), part(1)


PLANES = 4
LAYER_PARTS = 1
GATHER = (
    (1, 1, 0, 0), (1, 0, 0, 0), (1, 0, 0, -1), (3, 0, 0, 0), (2, 1, 0, 0), (2, 0, 0, 0), (1, 0, 0, 1), (4, 1, 0, 0), (1, 0, 0, 2), (3, 1, 0, 0),
    (1, 0, 0, -2), (2, 0, 0, -1), (3, 1, 0, 1), (4, 0, 0, 0), (2, 0, 0, 1), (4, 1, 0, -1), (3, 1, 0, -1), (1, 0, 0, 3), (4, 1, 0, 1), (2, 1, 0, 1),
    (3, 0, 0, -1), (1, 0, 0, -3), (1, 1, 0, 1), (5, 0, 0), (2, 1, 0, -1), (0, 0), (3, 0, 0, 1), (1, 1, 0, -1), (3, 0, 0, 2), (5, 1, 0), (2, 0, 0, -2),
    (4, 0, 0, -1), (5, 1, 1), (2, 0, 0, 2), (3, 1, 0, 2), (5, 1, -1), (3, 0, 0, -2), (2, 0, 0, -3), (3, 0, 0, -3), (3, 1, 0, -2), (4, 1, 0, -2),
    (4, 0, 0, 1), (2, 1, 0, 2), (1, 1, 0, 2), (4, 1, 0, 2), (5, 0, -1), (2, 0, 0, 3), (4, 0, 0, -2), (1, 1, 0, -2), (2, 1, 0, -2), (4, 0, 0, -3),
    (5, 0, 1), (5, 0, -2), (5, 0, -3), (0, 1), (0, 2), (0, 3), (4, 0, 0, 2), (5, 1, -2), (5, 1, 2), (0, 4), (2, 1, 0, -3), (3, 0, 0, 3), (4, 0, 0, 3),
    (0, 5), (5, 0, 2), (1, 1, 0, 3), (0, 6), (3, 1, 0, 3), (4, 1, 0, 3), (0, 7), (2, 1, 0, 3), (1, 1, 0, -3), (4, 1, 0, -3), (3, 1, 0, -3), (0, 8),
    (5, 0, 3), (0, 9), (5, 1, -3), (5, 1, 3), (0, 10),
)
SCATTER = (
    (1, 1, 0, 3, 0), (1, 1, 0, 2, 1), (1, 1, 0, 3, 1), (1, 1, 0, 0, 1), (1, 1, 0, 1, 1), (0, 0), (0, 1), (1, 0, 1, 3, 1), (1, 0, 0, 3, 1),
    (1, 0, 1, 3, 0), (1, 1, 0, 2, 0), (0, 2), (1, 1, 0, 1, 0), (2, 1, 0, 2, 0), (2, 1, 0, 1, 0), (0, 3), (0, 4), (2, 0, 0, 3, 0), (1, 1, 0, 0, 0),
    (0, 5), (1, 0, 0, 2, 0), (1, 0, 0, 2, 1), (1, 0, 2, 2, 0), (2, 1, 0, 3, 0), (0, 6), (2, 1, 0, 0, 0), (1, 0, 2, 2, 1), (3, 1, 0, 2, (0, True)),
    (3, 1, 0, 1, (0, True)), (0, 7), (1, 0, 0, 3, 0), (1, 0, 2, 3, 1), (2, 0, 0, 2, 0), (1, 0, 2, 3, 0), (0, 8), (3, 1, 0, 3, (0, True)), (0, 9),
    (1, 0, 1, 2, 1), (0, 10), (3, 1, 0, 2, (0, False)), (2, 0, 2, 2, 0), (3, 1, 0, 2, (1, True)), (3, 0, 0, 3, (0, True)), (2, 0, 1, 3, 0),
    (1, 0, 1, 2, 0), (2, 0, 2, 3, 0), (0, 11), (3, 0, 0, 3, (1, True)), (3, 1, 0, 0, (0, False)), (2, 0, 1, 2, 0), (0, 12), (1, 0, 0, 0, 1),
    (3, 0, 0, 3, (2, True)), (3, 0, 2, 2, (0, False)), (3, 0, 2, 3, (0, True)), (1, 0, 0, 0, 0), (4, 1, 0, 2, 0), (1, 0, 1, 1, 1),
    (3, 1, 0, 3, (1, True)), (3, 1, 0, 1, (0, False)), (1, 0, 2, 0, 1), (3, 0, 1, 2, (0, False)), (3, 0, 0, 2, (0, False)), (3, 1, 0, 0, (1, False)),
    (2, 0, 0, 0, 0), (3, 0, 0, 2, (0, True)), (3, 0, 1, 3, (0, True)), (3, 0, 2, 3, (1, True)), (1, 0, 1, 0, 1), (3, 0, 2, 2, (0, True)),
    (1, 0, 2, 0, 0), (3, 0, 1, 2, (0, True)), (0, 13), (3, 0, 0, 2, (1, True)), (2, 0, 2, 0, 0), (1, 0, 1, 0, 0), (3, 0, 0, 0, (0, False)),
    (3, 0, 1, 3, (1, True)), (3, 1, 0, 3, (2, True)), (3, 1, 0, 0, (2, False)), (1, 0, 0, 1, 1), (1, 0, 0, 1, 0), (3, 0, 0, 0, (2, False)),
    (3, 0, 2, 0, (0, False)), (3, 0, 1, 2, (1, True)), (3, 1, 0, 1, (1, False)), (3, 0, 0, 0, (1, False)), (2, 0, 1, 0, 0), (0, 14),
    (3, 0, 2, 3, (2, True)), (2, 0, 0, 1, 0), (1, 0, 2, 1, 1), (3, 0, 1, 0, (0, False)), (3, 0, 2, 0, (2, False)), (1, 0, 1, 1, 0), (4, 1, 0, 1, 0),
    (3, 0, 2, 2, (1, True)), (3, 0, 2, 0, (1, False)), (3, 0, 1, 3, (2, True)), (3, 0, 1, 0, (1, False)), (3, 0, 1, 0, (2, False)), (2, 0, 1, 1, 0),
    (0, 15), (3, 0, 0, 1, (0, False)), (4, 0, 2, 3, 0), (2, 0, 2, 1, 0), (3, 0, 1, 1, (0, True)), (1, 0, 2, 1, 0), (3, 0, 1, 1, (0, False)),
    (3, 0, 0, 1, (1, False)), (4, 0, 0, 3, 0), (3, 0, 0, 1, (0, True)), (0, 16), (4, 0, 0, 2, 0), (4, 1, 0, 3, 0), (4, 0, 1, 1, 0),
    (3, 0, 2, 1, (0, True)), (3, 0, 1, 1, (1, False)), (4, 0, 0, 1, 0), (3, 0, 2, 1, (0, False)), (3, 0, 2, 1, (1, False)), (4, 0, 1, 2, 0),
    (4, 0, 1, 0, 0), (4, 0, 2, 1, 0), (4, 0, 0, 0, 0), (4, 1, 0, 0, 0), (4, 0, 2, 2, 0), (4, 0, 1, 3, 0), (4, 0, 2, 0, 0),
)


def local_layout():
    return ((D, 3 * D), (D, D), (D, FF), (FF, D), (FF,)) + ((D,),) * 8


def conv_layout():
    return ((RATE * D, D), (D,), (D,), (D,))


def unpack(packed, layout):
    offset = 0
    pieces = []
    for extent in layout:
        length = math.prod(extent)
        pieces.append(packed[offset : offset + length].reshape(extent))
        offset = offset + length
    return pieces


def normalize_parts(values):
    average = jnp.mean(values, axis=-1, keepdims=True)
    centred = values - average
    spread = jnp.mean(centred * centred, axis=-1, keepdims=True)
    scaling = lax.rsqrt(spread + EPSILON)
    return (centred * scaling, scaling)


def normal_back(grad_normed, normed, scaling):
    first_mean = jnp.mean(grad_normed, axis=-1, keepdims=True)
    second_mean = jnp.mean(grad_normed * normed, axis=-1, keepdims=True)
    return scaling * (grad_normed - first_mean - normed * second_mean)


def product(left, right):
    return jnp.dot(left, right, preferred_element_type=jnp.float32)


def rows_inner(left, right):
    return lax.dot_general(
        left, right, (((0,), (0,)), ((), ())), preferred_element_type=jnp.float32
    )


def times_transpose(left, right):
    return lax.dot_general(
        left, right, (((1,), (1,)), ((), ())), preferred_element_type=jnp.float32
    )


def gelu_exact(values):
    return jax.nn.gelu(values, approximate=False)


def gelu_grad(values, upstream):
    return jax.vjp(gelu_exact, values)[1](upstream)[0]


def window_scores(projected, segments_block):
    row_count = projected.shape[0]
    windows = row_count // WINDOW
    heads_view = projected.reshape(windows, WINDOW, 3, HEADS, HEAD_SIZE)
    queries = heads_view[:, :, 0]
    keys_all = heads_view[:, :, 1]
    values = heads_view[:, :, 2]
    scores = jnp.einsum(
        "bqhe,bkhe->bhqk", queries, keys_all, preferred_element_type=jnp.float32
    ) * HEAD_SIZE ** (-0.5)
    grouped = segments_block.reshape(windows, WINDOW)
    allowed = grouped[:, None, :, None] == grouped[:, None, None, :]
    return (jnp.where(allowed, scores, -1e30), queries, keys_all, values)


def forward_pass(characters_block, segments_block, local_weights, conv_weights):
    (
        qkv_weight,
        out_weight,
        in_weight,
        down_weight,
        in_bias,
        gain_one,
        shift_one,
        query_bias,
        value_bias,
        out_bias,
        gain_two,
        shift_two,
        down_bias,
    ) = local_weights
    conv_weight, conv_bias, gain_three, shift_three = conv_weights
    row_count = characters_block.shape[0]
    inputs = characters_block.astype(jnp.float32)
    norm_one, scale_one = normalize_parts(inputs)
    normed = (norm_one * gain_one + shift_one).astype(jnp.bfloat16)
    proj_bias = jnp.concatenate([query_bias, jnp.zeros_like(query_bias), value_bias])
    projected = (product(normed, qkv_weight) + proj_bias).astype(jnp.bfloat16)
    scores, queries, keys_all, values = window_scores(projected, segments_block)
    largest = jnp.max(scores, axis=-1, keepdims=True)
    raised = jnp.exp(scores - largest)
    totals = jnp.sum(raised, axis=-1, keepdims=True)
    log_totals = largest + jnp.log(totals)
    weights = (raised / totals).astype(jnp.bfloat16)
    attended = jnp.einsum("bhqk,bkhe->bqhe", weights, values, preferred_element_type=jnp.float32)
    context = attended.reshape(row_count, D).astype(jnp.bfloat16)
    after_attention = inputs + product(context, out_weight) + out_bias
    norm_two, scale_two = normalize_parts(after_attention)
    middle = (norm_two * gain_two + shift_two).astype(jnp.bfloat16)
    pre_act = product(middle, in_weight) + in_bias
    hidden = gelu_exact(pre_act).astype(jnp.bfloat16)
    after_feed = after_attention + product(hidden, down_weight) + down_bias
    grouped_rows = after_feed.astype(jnp.bfloat16).reshape(row_count // RATE, RATE * D)
    conv_pre = product(grouped_rows, conv_weight) + conv_bias
    norm_three, scale_three = normalize_parts(gelu_exact(conv_pre))
    molecules = (norm_three * gain_three + shift_three).astype(jnp.bfloat16)
    saved_state = (
        segments_block,
        norm_one,
        scale_one,
        normed,
        projected,
        log_totals,
        context,
        norm_two,
        scale_two,
        middle,
        pre_act,
        hidden,
        grouped_rows,
        conv_pre,
        norm_three,
        scale_three,
    )
    return (molecules, saved_state)


def backward_pass(cotangent_block, saved_state, local_weights, conv_weights):
    (
        qkv_weight,
        out_weight,
        in_weight,
        down_weight,
        in_bias,
        gain_one,
        shift_one,
        query_bias,
        value_bias,
        out_bias,
        gain_two,
        shift_two,
        down_bias,
    ) = local_weights
    conv_weight, conv_bias, gain_three, shift_three = conv_weights
    (
        segments_block,
        norm_one,
        scale_one,
        normed,
        projected,
        log_totals,
        context,
        norm_two,
        scale_two,
        middle,
        pre_act,
        hidden,
        grouped_rows,
        conv_pre,
        norm_three,
        scale_three,
    ) = saved_state
    row_count = normed.shape[0]
    windows = row_count // WINDOW
    upstream = cotangent_block.astype(jnp.float32)
    grad_gain_three = jnp.sum(upstream * norm_three, axis=0)
    grad_shift_three = jnp.sum(upstream, axis=0)
    grad_activated = normal_back(upstream * gain_three, norm_three, scale_three)
    grad_conv_pre = gelu_grad(conv_pre, grad_activated).astype(jnp.bfloat16)
    grad_conv_bias = jnp.sum(grad_conv_pre.astype(jnp.float32), axis=0)
    grad_conv_weight = rows_inner(grouped_rows, grad_conv_pre)
    grad_feed = times_transpose(grad_conv_pre, conv_weight).reshape(row_count, D)
    grad_down_bias = jnp.sum(grad_feed, axis=0)
    grad_branch = grad_feed.astype(jnp.bfloat16)
    grad_down_weight = rows_inner(hidden, grad_branch)
    grad_hidden = times_transpose(grad_branch, down_weight)
    grad_pre = gelu_grad(pre_act, grad_hidden).astype(jnp.bfloat16)
    grad_in_bias = jnp.sum(grad_pre.astype(jnp.float32), axis=0)
    grad_in_weight = rows_inner(middle, grad_pre)
    grad_middle = times_transpose(grad_pre, in_weight)
    grad_gain_two = jnp.sum(grad_middle * norm_two, axis=0)
    grad_shift_two = jnp.sum(grad_middle, axis=0)
    grad_attention = grad_feed + normal_back(grad_middle * gain_two, norm_two, scale_two)
    grad_out_bias = jnp.sum(grad_attention, axis=0)
    grad_attn_out = grad_attention.astype(jnp.bfloat16)
    grad_out_weight = rows_inner(context, grad_attn_out)
    grad_context = times_transpose(grad_attn_out, out_weight).astype(jnp.bfloat16)
    grad_heads = grad_context.reshape(windows, WINDOW, HEADS, HEAD_SIZE)
    scores, queries, keys_all, values = window_scores(projected, segments_block)
    probs = jnp.exp(scores - log_totals)
    weights = probs.astype(jnp.bfloat16)
    grad_weights = jnp.einsum(
        "bqhe,bkhe->bhqk", grad_heads, values, preferred_element_type=jnp.float32
    )
    row_terms = jnp.sum(probs * grad_weights, axis=-1, keepdims=True)
    grad_scores = (probs * (grad_weights - row_terms)).astype(jnp.bfloat16)
    grad_queries = jnp.einsum(
        "bhqk,bkhe->bqhe", grad_scores, keys_all, preferred_element_type=jnp.float32
    ) * HEAD_SIZE ** (-0.5)
    grad_keys = jnp.einsum(
        "bhqk,bqhe->bkhe", grad_scores, queries, preferred_element_type=jnp.float32
    ) * HEAD_SIZE ** (-0.5)
    grad_values = jnp.einsum(
        "bhqk,bqhe->bkhe", weights, grad_heads, preferred_element_type=jnp.float32
    )
    grad_proj = (
        jnp.stack([grad_queries, grad_keys, grad_values], axis=2)
        .reshape(row_count, 3 * D)
        .astype(jnp.bfloat16)
    )
    proj_sums = jnp.sum(grad_proj.astype(jnp.float32), axis=0)
    grad_query_bias = proj_sums[:D]
    grad_value_bias = proj_sums[2 * D :]
    grad_qkv_weight = rows_inner(normed, grad_proj)
    grad_normed = times_transpose(grad_proj, qkv_weight)
    grad_gain_one = jnp.sum(grad_normed * norm_one, axis=0)
    grad_shift_one = jnp.sum(grad_normed, axis=0)
    grad_inputs = grad_attention + normal_back(grad_normed * gain_one, norm_one, scale_one)
    local_grad = jnp.concatenate(
        [
            grad_qkv_weight.reshape(-1),
            grad_out_weight.reshape(-1),
            grad_in_weight.reshape(-1),
            grad_down_weight.reshape(-1),
            grad_in_bias,
            grad_gain_one,
            grad_shift_one,
            grad_query_bias,
            grad_value_bias,
            grad_out_bias,
            grad_gain_two,
            grad_shift_two,
            grad_down_bias,
        ]
    )
    conv_grad = jnp.concatenate(
        [grad_conv_weight.reshape(-1), grad_conv_bias, grad_gain_three, grad_shift_three]
    )
    return (grad_inputs, local_grad, conv_grad)


def plain_device(characters, segment_ids, cotangent, local_params, conv_params):
    devices = lax.axis_size("fsdp")
    local_shard = local_params.shape[0]
    conv_shard = conv_params.shape[0]
    local_pad = local_shard * devices - LOCAL_COUNT
    conv_pad = conv_shard * devices - CONV_COUNT
    local_total = jnp.zeros((1, local_shard), jnp.float32)
    conv_total = jnp.zeros((1, conv_shard), jnp.float32)
    molecule_list = []
    gradient_list = []
    for micro_index in range(MICRO):
        local_full, conv_full = (
            lax.all_gather(local_params, "fsdp", axis=0, tiled=True),
            lax.all_gather(conv_params, "fsdp", axis=0, tiled=True),
        )
        molecules, saved_state = forward_pass(
            characters[micro_index],
            segment_ids[micro_index],
            unpack(local_full, local_layout()),
            unpack(conv_full, conv_layout()),
        )
        local_full, conv_full = (
            lax.all_gather(local_params, "fsdp", axis=0, tiled=True),
            lax.all_gather(conv_params, "fsdp", axis=0, tiled=True),
        )
        grad_inputs, local_grad, conv_grad = backward_pass(
            cotangent[micro_index],
            saved_state,
            unpack(local_full, local_layout()),
            unpack(conv_full, conv_layout()),
        )
        local_table = jnp.concatenate([local_grad, jnp.zeros((local_pad,), jnp.float32)]).reshape(
            devices, local_shard
        )
        conv_table = jnp.concatenate([conv_grad, jnp.zeros((conv_pad,), jnp.float32)]).reshape(
            devices, conv_shard
        )
        local_part, conv_part = (
            lax.psum_scatter(local_table, "fsdp", scatter_dimension=0, tiled=True),
            lax.psum_scatter(conv_table, "fsdp", scatter_dimension=0, tiled=True),
        )
        local_total = local_total + local_part
        conv_total = conv_total + conv_part
        molecule_list.append(molecules)
        gradient_list.append(grad_inputs)
    return (
        jnp.stack(molecule_list),
        jnp.stack(gradient_list),
        local_total.reshape(-1),
        conv_total.reshape(-1),
    )


def fused_kernel(geo, rows, in_names, out_names, scratch_names, *refs):
    n_in, n_out = len(in_names), len(out_names)
    every = dict(zip(list(in_names) + list(out_names) + list(scratch_names), refs))
    me, core, z, sib, first, second = where_am_i()
    g = SimpleNamespace(n=geo.n, Z=geo.Z, geo=geo, me=me, core=core, z=z, sib=sib, first=first, second=second, rows=rows, mols=rows // RATE, **every)
    g.from_sib = (every["from_sib_l"], every["from_sib_c"])
    program(g)


def program(g):
    Z = g.Z
    start_gather(g)
    ag = Gather(g, (LAYER_PARTS, 1))
    own = [e for e in GATHER if e[0] == 1 and e[1] == 0 and e[3] == 0]
    for e in own: ag.event(*e)
    table = gather_table(g)
    forward = [
        lambda: (same_segment(g), forward_norm(g)), lambda: forward_qkv(g, 0, 6), lambda: forward_qkv(g, 6, 9),
        lambda: forward_attention(g, 0, 12), lambda: forward_attention(g, 12, 24), lambda: forward_out(g),
        lambda: forward_up(g, 0, 4), lambda: forward_up(g, 4, 8), lambda: forward_up(g, 8, 12), lambda: forward_down(g), lambda: forward_conv(g)]
    for e in GATHER:
        if e[0] == 0: forward[e[1]]()
        elif e[0] == 5: ag.convert(*e[1:])
        elif e not in own: ag.event(*e)
    for e in GATHER:
        if 1 <= e[0] <= 4: ag.drain(*e)
    table()
    NL, NC = g.geo.RL // PART, g.geo.RC // PART
    conv_steps = [(1, p, zt) for zt in reversed(range(Z)) for p in range(NC)]
    layer_steps = [(0, p, zt) for zt in reversed(range(Z)) for p in range(NL)]
    names = {1: "second", 2: "first", 3: "line", 4: "last"}
    jobs = [(names[e[0]], e[1:4], e[4]) for e in SCATTER if e[0]]
    sc = Scatter(g, jobs)
    for zt in reversed(range(Z)):
        grad_conv_weight(g, zt)
        for st in conv_steps:
            if st[2] == zt: sc.p0(*st)
    def send_planes(lo, hi):
        sc.grant_all()
        for st in layer_steps:
            if lo <= st[2] < hi: sc.p0(*st)
    vec_stages = reduce_vectors(g)
    plane = 8 * g.geo.RL
    def plane_of(row): return -(-row // plane)
    q3, q2, q1 = plane_of(W2_ROW), plane_of(W1_ROW), plane_of(O_ROW)
    backward = [
        lambda: (back_conv(g), grad_down_weight(g, 0, 6)),
        lambda: (grad_down_weight(g, 6, 12), send_planes(q3, Z)),
        lambda: back_down(g, 0, 6),
        lambda: back_down(g, 6, 12),
        lambda: grad_up_weight(g, 0, 3),
        lambda: (grad_up_weight(g, 3, 6), send_planes(q2, q3)),
        lambda: back_up(g),
        lambda: (grad_out_weight(g), send_planes(q1, q2), back_out(g)),
        lambda: back_attention(g, 0, 1),
        lambda: back_attention(g, 1, 2),
        lambda: back_attention(g, 2, 3),
        lambda: back_attention(g, 3, 4),
        lambda: (grad_qkv_weight(g), send_planes(0, q1)),
        lambda: (back_qkv(g), pltpu.make_async_copy(g.dc, g.cg, g.osem.at[0]).start(), vec_stages[0]()),
        lambda: vec_stages[1](),
        lambda: vec_stages[2](),
        lambda: vec_stages[3](),
    ]
    for e in SCATTER:
        if e[0] == 0: backward[e[1]]()
        else: sc.run()
    layer, conv = place_gradients(g)
    layer[0]()
    conv[0]()
    layer[1]()
    conv[1]()
    layer[2]()
    conv[2]()
    for st in conv_steps + layer_steps: sc.finish(*st)
    pltpu.make_async_copy(g.dc, g.cg, g.osem.at[0]).wait()


def fused(n, characters, segment_ids, cotangent, local_params, conv_params):
    geo = Geo(n, local_params.shape[0], conv_params.shape[0])
    micro, span, _ = characters.shape
    rows = micro * span
    x = characters.reshape(rows, D)
    cot = cotangent.reshape(rows // RATE, D)
    xl = jnp.pad(local_params, (0, geo.XL * LANE - local_params.shape[0])).reshape(geo.XL, LANE)
    xc = jnp.pad(conv_params, (0, geo.XC * LANE - conv_params.shape[0])).reshape(geo.XC, LANE)
    V = pl.BlockSpec(memory_space=pltpu.VMEM)
    A = pl.BlockSpec(memory_space=pl.ANY)
    S = jax.ShapeDtypeStruct
    Z, H = geo.Z, geo.HL + geo.HC
    ins = dict(x=x, seg=segment_ids, cot=cot, xl=xl, xc=xc)
    outs = dict(mol=(V, S((rows // RATE, D), BF16)), cg=(A, S((rows, D), F32)), outl=(V, S((-(-geo.XL // 96) * 96, LANE), F32)), outc=(V, S((-(-geo.XC // 96) * 96, LANE), F32)))
    for name, count in (("from_sib", n // 2),):
        outs[name + "_l"] = (A, S((count * geo.RL, LANE), BF16))
        outs[name + "_c"] = (A, S((count * geo.RC, LANE), BF16))
    W = pltpu.VMEM
    DMA = pltpu.SemaphoreType.DMA
    sc = state_shapes(rows)
    sc.update(wqkv=W((D, 3 * D), BF16), wo=W((D, D), BF16), w1=W((D, FF), BF16), w2=W((FF, D), BF16), wc=W((FF, D), BF16))
    sc.update(gl=W((n * geo.RL, LANE), BF16), gc=W((n * geo.RC, LANE), BF16), hb=W((H, LANE), BF16), hr=W((H, LANE), BF16), tail=W((H, LANE), BF16),
              xlf=W((geo.HL + -(-geo.XL // 96) * 96 + 32, LANE), F32), xcf=W((geo.HC + -(-geo.XC // 96) * 96 + 32, LANE), F32), vgrad=W((H, LANE), F32), vland=W((4, H, LANE), F32),
              fs=W((H, LANE), F32), fr=W((H, LANE), F32), tmp=W((RING, PART, LANE), BF16), below_l=W((geo.RL, LANE), BF16), below_c=W((geo.RC, LANE), BF16))
    parts = (geo.RL + geo.RC) // PART
    sc.update(rsem=DMA((LAYER_PARTS + 1, n)), ssem=DMA((LAYER_PARTS + 1, 13 * Z)), hsem=DMA((6,)), tsem=DMA((5,)), osem=DMA((1,)), vsem=DMA((5,)), fsem=DMA((RING,)), credit=pltpu.SemaphoreType.REGULAR((5, (geo.RL + geo.RC) // PART * Z)),
              r_sib=DMA((parts, n // 2)), s_sib=DMA((parts, n // 2)), r_second=DMA((parts, 2 * Z)), s_second=DMA((parts, 2 * Z)),
              r_first=DMA((parts, Z)), s_first=DMA((parts, Z)), r_up=DMA((parts, Z)), s_up=DMA((parts, Z)), r_down=DMA((parts, Z)), s_down=DMA((parts, Z)))
    res = pl.pallas_call(
        functools.partial(fused_kernel, geo, rows, list(ins), list(outs), list(sc)),
        out_shape=[s for _, s in outs.values()],
        in_specs=[V] * len(ins),
        out_specs=[b for b, _ in outs.values()],
        scratch_shapes=list(sc.values()),
        compiler_params=pltpu.CompilerParams(collective_id=0, has_side_effects=True, vmem_limit_bytes=64 << 20),
        name="layer",
    )(*ins.values())
    mol, cg, outl, outc = res[:4]
    return (mol.reshape(micro, span // RATE, D), cg.reshape(micro, span, D), outl.reshape(-1)[:local_params.shape[0]], outc.reshape(-1)[:conv_params.shape[0]])


def on_device(characters, segment_ids, cotangent, local_params, conv_params):
    n = lax.axis_size("fsdp")
    rows = characters.shape[0] * characters.shape[1]
    whole = n // 8 == PLANES and n % 8 == 0 and (2 * 72 * D) % (n * UNIT) == 0 and (2 * 24 * D) % (n * UNIT) == 0
    exact = local_params.shape[0] * n == LOCAL_COUNT and conv_params.shape[0] * n == CONV_COUNT
    if whole and exact and rows == 4 * WINDOW:
        return fused(n, characters, segment_ids, cotangent, local_params, conv_params)
    return plain_device(characters, segment_ids, cotangent, local_params, conv_params)


def solution(mesh):
    return jax.shard_map(
        on_device,
        mesh=mesh,
        in_specs=(P(None, "fsdp", None), P(None, "fsdp"), P(None, "fsdp", None), P("fsdp"), P("fsdp")),
        out_specs=(P(None, "fsdp", None), P(None, "fsdp", None), P("fsdp"), P("fsdp")),
        check_vma=False,
    )
```

profile of v0, /device:TPU:15, one launch (start us, length us, event | category | flops | bytes accessed | tf_op | source)
XLA Modules:
  0.0 234.1 jit_solution(9500571706817410451)
XLA Ops:
  0.6 1.6 pad_bitcast_fusion.1.refs_4_
  2.2 1.8 pad_bitcast_fusion.refs_3_
  4.0 224.2 %layer.1 = (bf16[128,768]{1,0:T(8,128)(2,1)}, f32[512,768]{1,0:T(8,128)}, f32[1824,128]{1,0:T(8,128)}, f32[672,128]{1,0:T(8,128)}, bf16[27648,128]{1,0:T(8,128)(2,1)}, /*index=5*/bf16[9216,128]{1,0:T(8,128)(2,1)}) custom-call(bf16[512,768]{1,0:T(8,128)(2,1)} %bitcast.12, s32[2,256]{1,0:T(2,128)} %refs_1_.1, bf16[128,768]{1,0:T(8,128)(2,1)} %bitcast.14, ...), custom_call_target="tpu_custom_call" | custom-call | tf_op jit(solution)/shard_map/layer/pallas_call | solution.py:1195
  228.2 0.0 copy-start.1
  228.3 0.0 copy-start
  228.3 1.8 slice.9
  230.1 2.1 slice.8
  232.2 0.0 copy-done.1
  232.2 0.7 copy.11
  232.9 0.0 copy-done
  232.9 1.1 copy.12
Async XLA Ops:
  228.2 4.0 %copy-start.1 = (bf16[128,768]{1,0:T(8,128)(2,1)S(1)}, bf16[128,768]{1,0:T(8,128)(2,1)}, u32[]{:S(2)}) copy-start(bf16[128,768]{1,0:T(8,128)(2,1)} %get-tuple-element.8) | copy-start | bytes 589828
  228.3 4.7 %copy-start = (f32[512,768]{1,0:T(8,128)S(1)}, f32[512,768]{1,0:T(8,128)}, u32[]{:S(2)}) copy-start(f32[512,768]{1,0:T(8,128)} %get-tuple-element.9) | copy-start | bytes 4718596
where the time goes:
time: 235 us; the launch traced here: 234 us
  Pallas kernels  224 us (95%)
  local copies, waits for them, and re-layouts  9.18 us (4%)
    pallas_call x1, Pallas kernels, fused(): pl.pallas_call(functools.partial(fused_kernel, geo, rows, list(ins), list...  224 us

commit v1 on v0

--- a/solution.py
+++ b/solution.py
@@ -508,6 +508,10 @@
         self.jobs = jobs
         self.started, self.granted, self.waiting = set(), set(), []
         self.opened = self.closed = 0
+        self.arrived = set()
+        self.leads = {}
+        for kind, step, x in jobs:
+            if kind == "second": self.leads.setdefault(step, x)
 
     def target(self, zt, f, s):
         g = self.g
@@ -526,9 +530,12 @@
 
     def at(self, k, p, t): return self.own[k].at[self.rows(k, t, p)]
 
-    def to_sib(self, k, p, t):
+    def to_sib(self, k, p, zt):
         g = self.g
-        return self.move(self.at(k, p, t), g.from_sib[k].at[self.rows(k, t // 2, p)], g.s_sib, g.r_sib, self.sem(k, p), t // 2, g.sib)
+        half, size, part = g.n // 2, self.size[k], pl.ds(p * PART, PART)
+        src = self.own[k].reshape(half, 2, size, LANE).at[pl.ds(4 * zt, 4), 1 - g.core, part]
+        dst = g.from_sib[k].reshape(half, size, LANE).at[pl.ds(4 * zt, 4), part]
+        return self.move(src, dst, g.s_sib, g.r_sib, self.sem(k, p), zt, g.sib)
 
     def to_second(self, k, p, zt, f):
         g = self.g
@@ -550,9 +557,7 @@
         return self.move(self.at(k, p, self.target(zt, 0, 0)), dst, g.s_up, g.r_up, self.sem(k, p), zt, g.me + 8)
 
     def p0(self, k, p, zt):
-        for f in (0, 1):
-            for s in (0, 1):
-                self.to_sib(k, p, self.other(zt, f, s)).start()
+        self.to_sib(k, p, zt).start()
         self.started.add((k, p, zt))
         self.waiting.append((k, p, zt))
 
@@ -564,18 +569,15 @@
     def grant(self, k, p, zt):
         g = self.g
         z, Z, me = g.z, g.Z, g.me
-        for f in (0, 1):
-            for s in (0, 1):
-                self.to_sib(k, p, self.other(zt, f, s)).wait_send()
+        self.to_sib(k, p, zt).wait_send()
         self.credit(0, k, p, zt, g.second)
-        self.credit(1, k, p, zt, g.second)
-        self.credit(2, k, p, zt, g.first)
+        self.credit(1, k, p, zt, g.first)
         if zt < Z - 1:
             @pl.when(jnp.logical_and(z >= zt, z < Z - 1))
-            def _(): self.credit(3, k, p, zt, me + 8)
+            def _(): self.credit(2, k, p, zt, me + 8)
         if zt > 1:
             @pl.when(jnp.logical_and(z < zt, z > 0))
-            def _(): self.credit(4, k, p, zt, me - 8)
+            def _(): self.credit(3, k, p, zt, me - 8)
         self.granted.add((k, p, zt))
 
     def grant_all(self):
@@ -598,12 +600,12 @@
         z, Z, me = g.z, g.Z, g.me
         if kind == "second":
             def send():
-                self.spend(x, k, p, zt)
+                if self.leads[k, p, zt] == x: self.spend(0, k, p, zt)
                 self.to_second(k, p, zt, x).start()
             return [], [], None, send
         if kind == "first":
             def send():
-                self.spend(2, k, p, zt)
+                self.spend(1, k, p, zt)
                 self.to_first(k, p, zt).start()
             return [self.to_second(k, p, zt, 1)], [self.at(k, p, self.other(zt, 1, 0))], None, send
         waits = [self.to_second(k, p, zt, 0), self.to_first(k, p, zt)]
@@ -624,10 +626,10 @@
         here = hop if upward else Z - 1 - hop
         def send():
             if upward:
-                if here + 1 < zt: self.spend(4, k, p, zt)
+                if here + 1 < zt: self.spend(3, k, p, zt)
                 self.up(k, p, zt, here + 1 == zt).start()
             else:
-                self.spend(3, k, p, zt)
+                self.spend(2, k, p, zt)
                 self.down(k, p, zt).start()
         return waits, lands, None, send
 
@@ -642,10 +644,10 @@
     def open(self, i):
         job = self.jobs[i]
         cond, t = self.place(job)
-        def fn():
-            self.to_sib(*job[1][:2], t).wait_recv()
-            self.fetch(job, t, i % RING).start()
-        self.guard(cond, fn)
+        if job[1] not in self.arrived:
+            self.to_sib(*job[1]).wait_recv()
+            self.arrived.add(job[1])
+        self.guard(cond, lambda: self.fetch(job, t, i % RING).start())
 
     def close(self, i):
         g, job, slot = self.g, self.jobs[i], i % RING
@@ -696,34 +698,24 @@
     def take(slot):
         cp(slot, g.sib).wait_recv()
         g.vgrad[...] = g.vgrad[...] + g.vland[slot]
-    def give(slot, dev):
-        c = cp(slot, dev)
-        c.start()
-        c.wait_send()
+    def give(slot, dev): cp(slot, dev).start()
     on = core == 1
-    def stage0():
-        @pl.when(jnp.logical_not(on))
-        def _(): give(0, g.sib)
-        @pl.when(on)
-        def _(): take(0)
-    def stage1():
-        @pl.when(jnp.logical_and(on, bx == 0))
-        def _(): give(1, g.second)
-        @pl.when(jnp.logical_and(on, bx == 1))
-        def _(): take(1)
-    def stage2():
-        @pl.when(jnp.logical_and(on, jnp.logical_and(bx == 1, by == 0)))
-        def _(): give(2, g.first)
-        @pl.when(jnp.logical_and(on, jnp.logical_and(bx == 1, by == 1)))
-        def _(): take(2)
-    def stage3():
-        @pl.when(jnp.logical_and(on, jnp.logical_and(bx == 1, by == 1)))
-        def _():
-            @pl.when(z > 0)
-            def _(): take(3)
-            @pl.when(z < Z - 1)
-            def _(): give(3, me + 8)
-    return stage0, stage1, stage2, stage3
+    right = jnp.logical_and(on, bx == 1)
+    corner = jnp.logical_and(right, by == 1)
+    def stage(giver, taker, slot, dev):
+        def fn():
+            @pl.when(giver)
+            def _(): give(slot, dev)
+            @pl.when(taker)
+            def _(): take(slot)
+        return fn
+    stages = [stage(jnp.logical_not(on), on, 0, g.sib), stage(jnp.logical_and(on, bx == 0), right, 1, g.second),
+              stage(jnp.logical_and(right, by == 0), corner, 2, g.first)]
+    stages += [stage(jnp.logical_and(corner, z == h), jnp.logical_and(corner, z == h + 1), 3, me + 8) for h in range(Z - 1)]
+    def finish():
+        @pl.when(me != g.n - 1)
+        def _(): cp(0, g.sib).wait_send()
+    return stages, finish
 
 
 def place_gradients(g):
@@ -1086,6 +1078,9 @@
     )
 
 
+HOP_GAP = 8
+
+
 def fused_kernel(geo, rows, in_names, out_names, scratch_names, *refs):
     n_in, n_out = len(in_names), len(out_names)
     every = dict(zip(list(in_names) + list(out_names) + list(scratch_names), refs))
@@ -1127,7 +1122,7 @@
         sc.grant_all()
         for st in layer_steps:
             if lo <= st[2] < hi: sc.p0(*st)
-    vec_stages = reduce_vectors(g)
+    vec_stages, vec_finish = reduce_vectors(g)
     plane = 8 * g.geo.RL
     def plane_of(row): return -(-row // plane)
     q3, q2, q1 = plane_of(W2_ROW), plane_of(W1_ROW), plane_of(O_ROW)
@@ -1148,11 +1143,13 @@
         lambda: (back_qkv(g), pltpu.make_async_copy(g.dc, g.cg, g.osem.at[0]).start(), vec_stages[0]()),
         lambda: vec_stages[1](),
         lambda: vec_stages[2](),
-        lambda: vec_stages[3](),
+        vec_stages[3],
     ]
-    for e in SCATTER:
+    late = vec_stages[4:]
+    for i, e in enumerate(SCATTER):
         if e[0] == 0: backward[e[1]]()
         else: sc.run()
+        if late and i >= len(SCATTER) - 1 - HOP_GAP * (len(late) - 1): late.pop(0)()
     layer, conv = place_gradients(g)
     layer[0]()
     conv[0]()
@@ -1160,6 +1157,7 @@
     conv[1]()
     layer[2]()
     conv[2]()
+    vec_finish()
     for st in conv_steps + layer_steps: sc.finish(*st)
     pltpu.make_async_copy(g.dc, g.cg, g.osem.at[0]).wait()
 
@@ -1189,8 +1187,8 @@
               xlf=W((geo.HL + -(-geo.XL // 96) * 96 + 32, LANE), F32), xcf=W((geo.HC + -(-geo.XC // 96) * 96 + 32, LANE), F32), vgrad=W((H, LANE), F32), vland=W((4, H, LANE), F32),
               fs=W((H, LANE), F32), fr=W((H, LANE), F32), tmp=W((RING, PART, LANE), BF16), below_l=W((geo.RL, LANE), BF16), below_c=W((geo.RC, LANE), BF16))
     parts = (geo.RL + geo.RC) // PART
-    sc.update(rsem=DMA((LAYER_PARTS + 1, n)), ssem=DMA((LAYER_PARTS + 1, 13 * Z)), hsem=DMA((6,)), tsem=DMA((5,)), osem=DMA((1,)), vsem=DMA((5,)), fsem=DMA((RING,)), credit=pltpu.SemaphoreType.REGULAR((5, (geo.RL + geo.RC) // PART * Z)),
-              r_sib=DMA((parts, n // 2)), s_sib=DMA((parts, n // 2)), r_second=DMA((parts, 2 * Z)), s_second=DMA((parts, 2 * Z)),
+    sc.update(rsem=DMA((LAYER_PARTS + 1, n)), ssem=DMA((LAYER_PARTS + 1, 13 * Z)), hsem=DMA((6,)), tsem=DMA((5,)), osem=DMA((1,)), vsem=DMA((5,)), fsem=DMA((RING,)), credit=pltpu.SemaphoreType.REGULAR((4, (geo.RL + geo.RC) // PART * Z)),
+              r_sib=DMA((parts, Z)), s_sib=DMA((parts, Z)), r_second=DMA((parts, 2 * Z)), s_second=DMA((parts, 2 * Z)),
               r_first=DMA((parts, Z)), s_first=DMA((parts, Z)), r_up=DMA((parts, Z)), s_up=DMA((parts, Z)), r_down=DMA((parts, Z)), s_down=DMA((parts, Z)))
     res = pl.pallas_call(
         functools.partial(fused_kernel, geo, rows, list(ins), list(outs), list(sc)),

time: 235 us -> 228 us (0.970)
  Pallas kernels: 224 us -> 216 us
    pallas_call x1, Pallas kernels: 224 us -> 216 us  [fused(): pl.pallas_call(functools.partial(fused_kernel, geo, rows, list(ins), list...]
where the time goes in v1:
time: 228 us; the launch traced here: 226 us
  Pallas kernels  216 us (95%)
  local copies, waits for them, and re-layouts  9.18 us (4%)
    pallas_call x1, Pallas kernels, fused(): pl.pallas_call(functools.partial(fused_kernel, geo, rows, list(ins), list...  216 us

profile of v1, /device:TPU:15, one launch (start us, length us, event | category | flops | bytes accessed | tf_op | source)
XLA Modules:
  0.0 225.8 jit_solution(15795968216551254028)
XLA Ops:
  0.6 1.6 pad_bitcast_fusion.1.refs_4_
  2.2 1.8 pad_bitcast_fusion.refs_3_
  4.0 216.0 %layer.1 = (bf16[128,768]{1,0:T(8,128)(2,1)}, f32[512,768]{1,0:T(8,128)}, f32[1824,128]{1,0:T(8,128)}, f32[672,128]{1,0:T(8,128)}, bf16[27648,128]{1,0:T(8,128)(2,1)}, /*index=5*/bf16[9216,128]{1,0:T(8,128)(2,1)}) custom-call(bf16[512,768]{1,0:T(8,128)(2,1)} %bitcast.12, s32[2,256]{1,0:T(2,128)} %refs_1_.1, bf16[128,768]{1,0:T(8,128)(2,1)} %bitcast.14, ...), custom_call_target="tpu_custom_call" | custom-call | tf_op jit(solution)/shard_map/layer/pallas_call | solution.py:1193
  220.0 0.0 copy-start.1
  220.0 0.0 copy-start
  220.1 1.8 slice.9
  221.9 2.1 slice.8
  224.0 0.0 copy-done.1
  224.0 0.7 copy.11
  224.7 0.0 copy-done
  224.7 1.1 copy.12
Async XLA Ops:
  220.0 4.0 %copy-start.1 = (bf16[128,768]{1,0:T(8,128)(2,1)S(1)}, bf16[128,768]{1,0:T(8,128)(2,1)}, u32[]{:S(2)}) copy-start(bf16[128,768]{1,0:T(8,128)(2,1)} %get-tuple-element.8) | copy-start | bytes 589828
  220.0 4.7 %copy-start = (f32[512,768]{1,0:T(8,128)S(1)}, f32[512,768]{1,0:T(8,128)}, u32[]{:S(2)}) copy-start(f32[512,768]{1,0:T(8,128)} %get-tuple-element.9) | copy-start | bytes 4718596
